TPU v7x, 512 devices: a whole 4x8x8 slice. The times are simulated.
512 devices in a mesh: tm: 32 (over y_lo, z), fsdp: 16 (over x, y_hi, core).
Axes of the slice: x: 4, y: 8 (y_hi: 2, y_lo: 4; y = y_hi * 4 + y_lo), z: 8, core: 2. Of those that a mesh axis runs over, the one named last changes fastest.
Arguments:
- queries: bfloat16 [128, 512, 12, 128], P('tm', 'fsdp'), may hold values from -5 to 5
- key_states: bfloat16 [128, 512, 12, 128], P('tm', 'fsdp'), may hold values from -5 to 5
- value_states: bfloat16 [128, 512, 12, 128], P('tm', 'fsdp'), may hold values from -6 to 6
- out_grad: bfloat16 [128, 512, 3072], P('tm', 'fsdp'), may hold values from -6 to 6
- out_proj: bfloat16 [1536, 3072], P('fsdp'), may hold values from -0.109375 to 0.109375
Outputs:
- query_grad: bfloat16 [128, 512, 12, 128], P('tm', 'fsdp')
- key_grad: bfloat16 [128, 512, 12, 128], P('tm', 'fsdp')
- value_grad: bfloat16 [128, 512, 12, 128], P('tm', 'fsdp')
All inputs are finite; a program needn't handle non-finite values.
Results may differ from a plain program's by a relative error of at most 0.03.
Values may be sent and summed in bfloat16 or wider, within the bound.
A program may use at most 64 MiB of HBM per device.

v0:
```python
import jax
import jax.numpy as jnp
from jax import lax
from jax.sharding import PartitionSpec as P


def attend_back(query_block, key_block, value_block, grad_block):
    score_scale = query_block.shape[-1] ** (-0.5)
    scores = (
        jnp.einsum("fphd,gphd->phfg", query_block, key_block, preferred_element_type=jnp.float32)
        * score_scale
    )
    peak = jnp.max(scores, axis=-1, keepdims=True)
    expo = jnp.exp(scores - peak)
    probs = expo / jnp.sum(expo, axis=-1, keepdims=True)
    probs_b = probs.astype(jnp.bfloat16)
    attn_out = jnp.einsum(
        "phfg,gphd->fphd", probs_b, value_block, preferred_element_type=jnp.float32
    )
    row_delta = jnp.einsum("fphd,fphd->phf", grad_block.astype(jnp.float32), attn_out)
    dprobs = jnp.einsum(
        "fphd,gphd->phfg", grad_block, value_block, preferred_element_type=jnp.float32
    )
    dscores = (probs * (dprobs - row_delta[..., None])).astype(jnp.bfloat16)
    query_grad = (
        jnp.einsum("phfg,gphd->fphd", dscores, key_block, preferred_element_type=jnp.float32)
        * score_scale
    ).astype(jnp.bfloat16)
    key_grad = (
        jnp.einsum("phfg,fphd->gphd", dscores, query_block, preferred_element_type=jnp.float32)
        * score_scale
    ).astype(jnp.bfloat16)
    value_grad = jnp.einsum(
        "phfg,fphd->gphd", probs_b, grad_block, preferred_element_type=jnp.float32
    ).astype(jnp.bfloat16)
    return (query_grad, key_grad, value_grad)


def send_back(grads):
    return (
        lax.all_to_all(grads[0], "tm", split_axis=0, concat_axis=1, tiled=True),
        lax.all_to_all(grads[1], "tm", split_axis=0, concat_axis=1, tiled=True),
        lax.all_to_all(grads[2], "tm", split_axis=0, concat_axis=1, tiled=True),
    )


def body(queries, key_states, value_states, out_grad, out_proj):
    frames_dev, pos_dev, heads, head_size = queries.shape
    width = out_grad.shape[-1]
    flat = out_grad.reshape(frames_dev * pos_dev, width)
    grad_flat = lax.dot_general(
        flat,
        lax.all_gather(out_proj, "fsdp", axis=0, tiled=True),
        (((1,), (1,)), ((), ())),
        preferred_element_type=jnp.float32,
    ).astype(jnp.bfloat16)
    grad_attn = grad_flat.reshape(frames_dev, pos_dev, heads, head_size)
    results = send_back(
        attend_back(
            lax.all_to_all(queries, "tm", split_axis=1, concat_axis=0, tiled=True),
            lax.all_to_all(key_states, "tm", split_axis=1, concat_axis=0, tiled=True),
            lax.all_to_all(value_states, "tm", split_axis=1, concat_axis=0, tiled=True),
            lax.all_to_all(grad_attn, "tm", split_axis=1, concat_axis=0, tiled=True),
        )
    )
    return (results[0], results[1], results[2])


def solution(mesh):
    return jax.shard_map(
        body,
        mesh=mesh,
        in_specs=(
            P("tm", "fsdp", None, None),
            P("tm", "fsdp", None, None),
            P("tm", "fsdp", None, None),
            P("tm", "fsdp", None),
            P("fsdp", None),
        ),
        out_specs=(
            P("tm", "fsdp", None, None),
            P("tm", "fsdp", None, None),
            P("tm", "fsdp", None, None),
        ),
        check_vma=False,
    )
```

profile of v0, /device:TPU:64, one launch (start us, length us, event | category | flops | bytes accessed | tf_op | source)
XLA Modules:
  0.0 255.6 jit_solution(9501734445395635205)
XLA Ops:
  7.9 2.0 copy.39
  9.9 13.2 %all-to-all-start = ((bf16[4,32,12,128]{3,2,0,1:T(8,128)(2,1)}), bf16[4,32,12,128]{3,2,0,1:T(8,128)(2,1)S(1)}, u32[]{:S(2)}, u32[]{:S(2)}) async-start(bf16[4,32,12,128]{3,2,0,1:T(8,128)(2,1)} %copy.39), calls=%async_computation | async-start | bytes 1048576 | tf_op jit(solution)/shard_map/all_to_all | solution.py:60
  23.1 2.0 copy.41
  25.0 22.8 %all-to-all-done = bf16[4,32,12,128]{3,2,0,1:T(8,128)(2,1)S(1)} async-done(((bf16[4,32,12,128]{3,2,0,1:T(8,128)(2,1)}), bf16[4,32,12,128]{3,2,0,1:T(8,128)(2,1)S(1)}, u32[]{:S(2)}, u32[]{:S(2)}) %all-to-all-start) | async-done | bytes 393248 | tf_op jit(solution)/shard_map/all_to_all | solution.py:60
  47.8 6.2 %all-to-all-start.1 = ((bf16[4,32,12,128]{3,2,0,1:T(8,128)(2,1)}), bf16[4,32,12,128]{3,2,0,1:T(8,128)(2,1)S(1)}, u32[]{:S(2)}, u32[]{:S(2)}) async-start(bf16[4,32,12,128]{3,2,0,1:T(8,128)(2,1)} %copy.41), calls=%async_computation.1 | async-start | bytes 1048576 | tf_op jit(solution)/shard_map/all_to_all | solution.py:61
  54.0 2.0 copy.45
  56.0 14.3 %all-to-all-done.1 = bf16[4,32,12,128]{3,2,0,1:T(8,128)(2,1)S(1)} async-done(((bf16[4,32,12,128]{3,2,0,1:T(8,128)(2,1)}), bf16[4,32,12,128]{3,2,0,1:T(8,128)(2,1)S(1)}, u32[]{:S(2)}, u32[]{:S(2)}) %all-to-all-start.1) | async-done | bytes 393248 | tf_op jit(solution)/shard_map/all_to_all | solution.py:61
  70.3 4.7 %all-to-all-start.3 = ((bf16[4,32,12,128]{3,2,0,1:T(8,128)(2,1)}), bf16[4,32,12,128]{3,2,0,1:T(8,128)(2,1)S(1)}, u32[]{:S(2)}, u32[]{:S(2)}) async-start(bf16[4,32,12,128]{3,2,0,1:T(8,128)(2,1)} %copy.45), calls=%async_computation.3 | async-start | bytes 1048576 | tf_op jit(solution)/shard_map/all_to_all | solution.py:62
  75.0 71.0 %all-gather.2.cloned.1.call-done = bf16[1536,3072]{1,0:T(8,128)(2,1)} async-done(((bf16[96,3072]{1,0:T(8,128)(2,1)}), bf16[1536,3072]{1,0:T(8,128)(2,1)}) %all-gather.2.cloned.1.call-update) | async-done | bytes 9437200 | tf_op jit(solution)/shard_map/all_gather | solution.py:53
  146.0 6.9 %convolution_convert_fusion = bf16[128,1536]{1,0:T(8,128)(2,1)S(1)} fusion(bf16[128,3072]{1,0:T(8,128)(2,1)S(1)} %bitcast.71, bf16[1536,3072]{1,0:T(8,128)(2,1)} %all-gather.2.cloned.1.call-done), kind=kOutput, calls=%fused_computation.1 | convolution fusion | flops 1208156160 | bytes 10616832 | tf_op jit(solution)/shard_map/dot_general | solution.py:51
  153.2 1.1 copy.43
  154.3 8.0 %all-to-all-start.2 = ((bf16[4,32,12,128]{3,0,2,1:T(4,128)(2,1)}), bf16[4,32,12,128]{3,0,2,1:T(4,128)(2,1)S(1)}, u32[]{:S(2)}, u32[]{:S(2)}) async-start(bf16[4,32,12,128]{3,0,2,1:T(4,128)(2,1)} %copy.43), calls=%async_computation.2 | async-start | bytes 786432 | tf_op jit(solution)/shard_map/all_to_all | solution.py:63
  163.2 14.1 %all-to-all-done.2 = bf16[4,32,12,128]{3,0,2,1:T(4,128)(2,1)S(1)} async-done(((bf16[4,32,12,128]{3,0,2,1:T(4,128)(2,1)}), bf16[4,32,12,128]{3,0,2,1:T(4,128)(2,1)S(1)}, u32[]{:S(2)}, u32[]{:S(2)}) %all-to-all-start.2) | async-done | bytes 393248 | tf_op jit(solution)/shard_map/all_to_all | solution.py:63
  178.0 1.5 fusion.4
  179.9 1.2 copy.51
  181.1 4.7 %all-to-all-start.4 = ((bf16[128,1,12,128]{3,2,1,0:T(8,128)(2,1)}), bf16[128,1,12,128]{3,2,1,0:T(8,128)(2,1)S(1)}, u32[]{:S(2)}, u32[]{:S(2)}) async-start(bf16[128,1,12,128]{3,2,1,0:T(8,128)(2,1)} %copy.51), calls=%async_computation.4 | async-start | bytes 1048576 | tf_op jit(solution)/shard_map/all_to_all | solution.py:41
  186.2 1.2 copy.54
  187.4 15.8 %all-to-all-done.4 = bf16[128,1,12,128]{3,2,1,0:T(8,128)(2,1)S(1)} async-done(((bf16[128,1,12,128]{3,2,1,0:T(8,128)(2,1)}), bf16[128,1,12,128]{3,2,1,0:T(8,128)(2,1)S(1)}, u32[]{:S(2)}, u32[]{:S(2)}) %all-to-all-start.4) | async-done | bytes 393248 | tf_op jit(solution)/shard_map/all_to_all | solution.py:41
  203.2 4.7 %all-to-all-start.5 = ((bf16[128,1,12,128]{3,2,1,0:T(8,128)(2,1)}), bf16[128,1,12,128]{3,2,1,0:T(8,128)(2,1)S(1)}, u32[]{:S(2)}, u32[]{:S(2)}) async-start(bf16[128,1,12,128]{3,2,1,0:T(8,128)(2,1)} %copy.54), calls=%async_computation.5 | async-start | bytes 1048576 | tf_op jit(solution)/shard_map/all_to_all | solution.py:42
  208.0 1.6 fusion.8
  209.5 1.2 copy.58
  210.7 14.8 %all-to-all-done.5 = bf16[128,1,12,128]{3,2,1,0:T(8,128)(2,1)S(1)} async-done(((bf16[128,1,12,128]{3,2,1,0:T(8,128)(2,1)}), bf16[128,1,12,128]{3,2,1,0:T(8,128)(2,1)S(1)}, u32[]{:S(2)}, u32[]{:S(2)}) %all-to-all-start.5) | async-done | bytes 393248 | tf_op jit(solution)/shard_map/all_to_all | solution.py:42
  225.5 4.7 %all-to-all-start.6 = ((bf16[128,1,12,128]{3,2,1,0:T(8,128)(2,1)}), bf16[128,1,12,128]{3,2,1,0:T(8,128)(2,1)S(1)}, u32[]{:S(2)}, u32[]{:S(2)}) async-start(bf16[128,1,12,128]{3,2,1,0:T(8,128)(2,1)} %copy.58), calls=%async_computation.6 | async-start | bytes 1048576 | tf_op jit(solution)/shard_map/all_to_all | solution.py:43
  232.1 15.7 %all-to-all-done.6 = bf16[128,1,12,128]{3,2,1,0:T(8,128)(2,1)S(1)} async-done(((bf16[128,1,12,128]{3,2,1,0:T(8,128)(2,1)}), bf16[128,1,12,128]{3,2,1,0:T(8,128)(2,1)S(1)}, u32[]{:S(2)}, u32[]{:S(2)}) %all-to-all-start.6) | async-done | bytes 393248 | tf_op jit(solution)/shard_map/all_to_all | solution.py:43
  (22 shorter events, 6.1 us)
Async XLA Ops:
  7.2 138.8 %copy-start = (bf16[4,32,3072]{2,1,0:T(8,128)(2,1)S(1)}, bf16[4,32,3072]{2,1,0:T(8,128)(2,1)}, u32[]{:S(2)}) copy-start(bf16[4,32,3072]{2,1,0:T(8,128)(2,1)} %param.8) | copy-start | bytes 2359300
  7.2 138.8 %all-gather.2.cloned.1.call-start = ((), (), s32[]{:S(2)}) async-start(), calls=%async_computation.7 | async-start | bytes 10027008 | tf_op jit(solution)/shard_map/all_gather | solution.py:53
  9.9 37.9 %all-to-all-start = ((bf16[4,32,12,128]{3,2,0,1:T(8,128)(2,1)}), bf16[4,32,12,128]{3,2,0,1:T(8,128)(2,1)S(1)}, u32[]{:S(2)}, u32[]{:S(2)}) async-start(bf16[4,32,12,128]{3,2,0,1:T(8,128)(2,1)} %copy.39), calls=%async_computation | async-start | bytes 1048576 | tf_op jit(solution)/shard_map/all_to_all | solution.py:60
  47.8 22.5 %all-to-all-start.1 = ((bf16[4,32,12,128]{3,2,0,1:T(8,128)(2,1)}), bf16[4,32,12,128]{3,2,0,1:T(8,128)(2,1)S(1)}, u32[]{:S(2)}, u32[]{:S(2)}) async-start(bf16[4,32,12,128]{3,2,0,1:T(8,128)(2,1)} %copy.41), calls=%async_computation.1 | async-start | bytes 1048576 | tf_op jit(solution)/shard_map/all_to_all | solution.py:61
  70.3 84.0 %all-to-all-start.3 = ((bf16[4,32,12,128]{3,2,0,1:T(8,128)(2,1)}), bf16[4,32,12,128]{3,2,0,1:T(8,128)(2,1)S(1)}, u32[]{:S(2)}, u32[]{:S(2)}) async-start(bf16[4,32,12,128]{3,2,0,1:T(8,128)(2,1)} %copy.45), calls=%async_computation.3 | async-start | bytes 1048576 | tf_op jit(solution)/shard_map/all_to_all | solution.py:62
  154.3 23.1 %all-to-all-start.2 = ((bf16[4,32,12,128]{3,0,2,1:T(4,128)(2,1)}), bf16[4,32,12,128]{3,0,2,1:T(4,128)(2,1)S(1)}, u32[]{:S(2)}, u32[]{:S(2)}) async-start(bf16[4,32,12,128]{3,0,2,1:T(4,128)(2,1)} %copy.43), calls=%async_computation.2 | async-start | bytes 786432 | tf_op jit(solution)/shard_map/all_to_all | solution.py:63
  163.2 14.7 %copy-start.1 = (f32[12,128,128]{1,2,0:T(8,128)}, f32[12,128,128]{1,2,0:T(8,128)S(1)}, u32[]{:S(2)}) copy-start(f32[12,128,128]{1,2,0:T(8,128)S(1)} %get-tuple-element.10) | copy-start | bytes 2359300
  181.1 22.2 %all-to-all-start.4 = ((bf16[128,1,12,128]{3,2,1,0:T(8,128)(2,1)}), bf16[128,1,12,128]{3,2,1,0:T(8,128)(2,1)S(1)}, u32[]{:S(2)}, u32[]{:S(2)}) async-start(bf16[128,1,12,128]{3,2,1,0:T(8,128)(2,1)} %copy.51), calls=%async_computation.4 | async-start | bytes 1048576 | tf_op jit(solution)/shard_map/all_to_all | solution.py:41
  203.2 22.3 %all-to-all-start.5 = ((bf16[128,1,12,128]{3,2,1,0:T(8,128)(2,1)}), bf16[128,1,12,128]{3,2,1,0:T(8,128)(2,1)S(1)}, u32[]{:S(2)}, u32[]{:S(2)}) async-start(bf16[128,1,12,128]{3,2,1,0:T(8,128)(2,1)} %copy.54), calls=%async_computation.5 | async-start | bytes 1048576 | tf_op jit(solution)/shard_map/all_to_all | solution.py:42
  225.5 22.3 %all-to-all-start.6 = ((bf16[128,1,12,128]{3,2,1,0:T(8,128)(2,1)}), bf16[128,1,12,128]{3,2,1,0:T(8,128)(2,1)S(1)}, u32[]{:S(2)}, u32[]{:S(2)}) async-start(bf16[128,1,12,128]{3,2,1,0:T(8,128)(2,1)} %copy.58), calls=%async_computation.6 | async-start | bytes 1048576 | tf_op jit(solution)/shard_map/all_to_all | solution.py:43
Sparse Core Ops, SparseCore 0:
  11.3 134.6 all-gather.1
where the time goes:
time: 257 us; the launch traced here: 256 us
  waiting for transfers between devices  169 us (66%)
  starting transfers between devices  46.3 us (18%)
  local copies, waits for them, and re-layouts  14.3 us (6%)
  between operations  14.2 us (6%)
  matrix products  11.7 us (5%)
    all_gather x1, waiting for transfers between devices, body(): lax.all_gather(out_proj, 'fsdp', axis=0, tiled=True)  71 us
    all_to_all x1, waiting for transfers between devices, body(): lax.all_to_all(queries, 'tm', split_axis=1, concat_axis=0, tiled=True)  22.8 us
    all_to_all x1, waiting for transfers between devices, send_back(): lax.all_to_all(grads[0], 'tm', split_axis=0, concat_axis=1, tiled=True)  15.8 us
    all_to_all x1, waiting for transfers between devices, send_back(): lax.all_to_all(grads[2], 'tm', split_axis=0, concat_axis=1, tiled=True)  15.7 us
    all_to_all x1, waiting for transfers between devices, send_back(): lax.all_to_all(grads[1], 'tm', split_axis=0, concat_axis=1, tiled=True)  14.8 us
    all_to_all x1, waiting for transfers between devices, body(): lax.all_to_all(key_states, 'tm', split_axis=1, concat_axis=0, tiled=True)  14.3 us
    all_to_all x1, waiting for transfers between devices, body(): lax.all_to_all(grad_attn, 'tm', split_axis=1, concat_axis=0, tiled=True)  14.1 us
    all_to_all x1, starting transfers between devices, body(): lax.all_to_all(queries, 'tm', split_axis=1, concat_axis=0, tiled=True)  13.2 us
  transfers between devices with their start and end apart: 8, of which 7 were waited for; matrix products, arithmetic and copies ran while one was open for 8% of the time, Pallas kernels for 0%

commit v1 on v0

--- a/solution.py
+++ b/solution.py
@@ -50,7 +50,9 @@
     flat = out_grad.reshape(frames_dev * pos_dev, width)
     grad_flat = lax.dot_general(
         flat,
-        lax.all_gather(out_proj, "fsdp", axis=0, tiled=True),
+        jnp.concatenate(
+            lax.all_to_all(jnp.stack([out_proj] * lax.axis_size("fsdp")), "fsdp", 0, 0), axis=0
+        ),
         (((1,), (1,)), ((), ())),
         preferred_element_type=jnp.float32,
     ).astype(jnp.bfloat16)

time: 257 us -> 412 us (1.60)
  waiting for transfers between devices: 169 us -> 295 us
  blocking collectives: 0 us -> 22.1 us
  starting transfers between devices: 46.3 us -> 60.8 us
  between operations: 14.2 us -> 0.8 us
  local copies, waits for them, and re-layouts: 14.3 us -> 18.5 us
    all_to_all x1, waiting for transfers between devices: 22.8 us -> 211 us  [body(): lax.all_to_all(jnp.stack([out_proj] * lax.axis_size('fsdp')), 'fsdp', 0, 0)]
    all_gather x1 -> x0, waiting for transfers between devices: 71 us -> none  [body(): lax.all_gather(out_proj, 'fsdp', axis=0, tiled=True)]
    all_to_all x0 -> x1, blocking collectives: none -> 22.1 us  [body(): lax.all_to_all(queries, 'tm', split_axis=1, concat_axis=0, tiled=True)]
    all_to_all x1, waiting for transfers between devices: 0.01 us -> 16.2 us  [body(): lax.all_to_all(value_states, 'tm', split_axis=1, concat_axis=0, tiled=True)]
    all_to_all x1, starting transfers between devices: 6.15 us -> 21.4 us  [body(): lax.all_to_all(key_states, 'tm', split_axis=1, concat_axis=0, tiled=True)]
    all_to_all x1, starting transfers between devices: 4.74 us -> 13.2 us  [body(): lax.all_to_all(value_states, 'tm', split_axis=1, concat_axis=0, tiled=True)]
    all_to_all x1, starting transfers between devices: 13.2 us -> 7.14 us  [body(): lax.all_to_all(jnp.stack([out_proj] * lax.axis_size('fsdp')), 'fsdp', 0, 0)]
    another operation x0 -> x1, local copies, waits for them, and re-layouts: none -> 5.92 us  [body(): jnp.stack([out_proj] * lax.axis_size('fsdp'))]
  transfers between devices with their start and end apart: 8 -> 7, of which waited for: 7 -> 7; matrix products, arithmetic and copies ran while one was open for 8% -> 4% of each run, Pallas kernels for 0% -> 0%
where the time goes in v1:
time: 412 us; the launch traced here: 411 us
  waiting for transfers between devices  295 us (72%)
  starting transfers between devices  60.8 us (15%)
  blocking collectives  22.1 us (5%)
  local copies, waits for them, and re-layouts  18.5 us (4%)
  matrix products  13.7 us (3%)
    all_to_all x1, waiting for transfers between devices, body(): lax.all_to_all(jnp.stack([out_proj] * lax.axis_size('fsdp')), 'fsdp', 0, 0)  211 us
    all_to_all x1, blocking collectives, body(): lax.all_to_all(queries, 'tm', split_axis=1, concat_axis=0, tiled=True)  22.1 us
    all_to_all x1, starting transfers between devices, body(): lax.all_to_all(key_states, 'tm', split_axis=1, concat_axis=0, tiled=True)  21.4 us
    all_to_all x1, waiting for transfers between devices, body(): lax.all_to_all(value_states, 'tm', split_axis=1, concat_axis=0, tiled=True)  16.2 us
    all_to_all x1, waiting for transfers between devices, send_back(): lax.all_to_all(grads[0], 'tm', split_axis=0, concat_axis=1, tiled=True)  15.8 us
    all_to_all x1, waiting for transfers between devices, send_back(): lax.all_to_all(grads[2], 'tm', split_axis=0, concat_axis=1, tiled=True)  15.7 us
    all_to_all x1, waiting for transfers between devices, send_back(): lax.all_to_all(grads[1], 'tm', split_axis=0, concat_axis=1, tiled=True)  14.7 us
    all_to_all x1, starting transfers between devices, body(): lax.all_to_all(value_states, 'tm', split_axis=1, concat_axis=0, tiled=True)  13.2 us
  transfers between devices with their start and end apart: 7, of which 7 were waited for; matrix products, arithmetic and copies ran while one was open for 4% of the time, Pallas kernels for 0%

profile of v1, /device:TPU:64, one launch (start us, length us, event | category | flops | bytes accessed | tf_op | source)
XLA Modules:
  0.0 410.7 jit_solution(4394333331313656781)
XLA Ops:
  0.6 2.0 copy.45
  2.7 13.2 %all-to-all-start.4 = ((bf16[4,32,12,128]{3,2,0,1:T(8,128)(2,1)}), bf16[4,32,12,128]{3,2,0,1:T(8,128)(2,1)S(1)}, u32[]{:S(2)}, u32[]{:S(2)}) async-start(bf16[4,32,12,128]{3,2,0,1:T(8,128)(2,1)} %copy.45), calls=%async_computation.4 | async-start | bytes 1048576 | tf_op jit(solution)/shard_map/all_to_all | solution.py:64
  17.0 16.2 %all-to-all-done.4 = bf16[4,32,12,128]{3,2,0,1:T(8,128)(2,1)S(1)} async-done(((bf16[4,32,12,128]{3,2,0,1:T(8,128)(2,1)}), bf16[4,32,12,128]{3,2,0,1:T(8,128)(2,1)S(1)}, u32[]{:S(2)}, u32[]{:S(2)}) %all-to-all-start.4) | async-done | bytes 393248 | tf_op jit(solution)/shard_map/all_to_all | solution.py:64
  33.2 22.1 %all_to_all.119 = bf16[4,32,12,128]{3,2,0,1:T(8,128)(2,1)S(1)} all-to-all(bf16[4,32,12,128]{3,2,0,1:T(8,128)(2,1)S(1)} %copy.39), channel_id=1, replica_groups=mesh['tm'=32,'fsdp'=16] {'tm'}, dimensions={1} | all-to-all | bytes 786432 | tf_op jit(solution)/shard_map/all_to_all | solution.py:62
  55.3 5.9 %stack.2 = bf16[16,96,3072]{2,1,0:T(8,128)(2,1)} broadcast(bf16[96,3072]{1,0:T(8,128)(2,1)} %param.9), dimensions={1,2} | broadcast | bytes 10027008 | tf_op jit(solution)/shard_map/stack | solution.py:54
  61.2 7.1 %all-to-all-start.2 = ((bf16[16,96,3072]{2,1,0:T(8,128)(2,1)}), bf16[16,96,3072]{2,1,0:T(8,128)(2,1)}, u32[]{:S(2)}, u32[]{:S(2)}) async-start(bf16[16,96,3072]{2,1,0:T(8,128)(2,1)} %stack.2), calls=%async_computation.2 | async-start | bytes 18874368 | tf_op jit(solution)/shard_map/all_to_all | solution.py:54
  69.4 210.7 %all-to-all-done.2 = bf16[16,96,3072]{2,1,0:T(8,128)(2,1)} async-done(((bf16[16,96,3072]{2,1,0:T(8,128)(2,1)}), bf16[16,96,3072]{2,1,0:T(8,128)(2,1)}, u32[]{:S(2)}, u32[]{:S(2)}) %all-to-all-start.2) | async-done | bytes 9437216 | tf_op jit(solution)/shard_map/all_to_all | solution.py:54
  280.1 21.4 %all-to-all-start.1 = ((bf16[4,32,12,128]{3,2,0,1:T(8,128)(2,1)}), bf16[4,32,12,128]{3,2,0,1:T(8,128)(2,1)S(1)}, u32[]{:S(2)}, u32[]{:S(2)}) async-start(bf16[4,32,12,128]{3,2,0,1:T(8,128)(2,1)} %copy.41), calls=%async_computation.1 | async-start | bytes 1048576 | tf_op jit(solution)/shard_map/all_to_all | solution.py:63
  301.5 6.9 %convolution_convert_fusion = bf16[128,1536]{1,0:T(8,128)(2,1)S(1)} fusion(bf16[128,3072]{1,0:T(8,128)(2,1)S(1)} %bitcast.72, bf16[1536,3072]{1,0:T(8,128)(2,1)} %bitcast.9), kind=kOutput, calls=%fused_computation.1 | convolution fusion | flops 1208156160 | bytes 10616832 | tf_op jit(solution)/shard_map/dot_general | solution.py:51
  309.8 8.9 %all-to-all-done.1 = bf16[4,32,12,128]{3,2,0,1:T(8,128)(2,1)S(1)} async-done(((bf16[4,32,12,128]{3,2,0,1:T(8,128)(2,1)}), bf16[4,32,12,128]{3,2,0,1:T(8,128)(2,1)S(1)}, u32[]{:S(2)}, u32[]{:S(2)}) %all-to-all-start.1) | async-done | bytes 393248 | tf_op jit(solution)/shard_map/all_to_all | solution.py:63
  318.6 4.9 %all-to-all-start.3 = ((bf16[4,32,12,128]{3,0,2,1:T(4,128)(2,1)}), bf16[4,32,12,128]{3,0,2,1:T(4,128)(2,1)S(1)}, u32[]{:S(2)}, u32[]{:S(2)}) async-start(bf16[4,32,12,128]{3,0,2,1:T(4,128)(2,1)} %copy.43), calls=%async_computation.3 | async-start | bytes 786432 | tf_op jit(solution)/shard_map/all_to_all | solution.py:65
  324.0 1.3 fusion.16
  325.3 12.8 %all-to-all-done.3 = bf16[4,32,12,128]{3,0,2,1:T(4,128)(2,1)S(1)} async-done(((bf16[4,32,12,128]{3,0,2,1:T(4,128)(2,1)}), bf16[4,32,12,128]{3,0,2,1:T(4,128)(2,1)S(1)}, u32[]{:S(2)}, u32[]{:S(2)}) %all-to-all-start.3) | async-done | bytes 393248 | tf_op jit(solution)/shard_map/all_to_all | solution.py:65
  338.4 1.6 fusion.7
  340.0 1.5 fusion.4
  343.0 4.7 %all-to-all-start.5 = ((bf16[128,1,12,128]{3,2,1,0:T(8,128)(2,1)}), bf16[128,1,12,128]{3,2,1,0:T(8,128)(2,1)S(1)}, u32[]{:S(2)}, u32[]{:S(2)}) async-start(bf16[128,1,12,128]{3,2,1,0:T(8,128)(2,1)} %copy.51), calls=%async_computation.5 | async-start | bytes 1048576 | tf_op jit(solution)/shard_map/all_to_all | solution.py:41
  348.2 1.2 copy.54
  349.4 15.8 %all-to-all-done.5 = bf16[128,1,12,128]{3,2,1,0:T(8,128)(2,1)S(1)} async-done(((bf16[128,1,12,128]{3,2,1,0:T(8,128)(2,1)}), bf16[128,1,12,128]{3,2,1,0:T(8,128)(2,1)S(1)}, u32[]{:S(2)}, u32[]{:S(2)}) %all-to-all-start.5) | async-done | bytes 393248 | tf_op jit(solution)/shard_map/all_to_all | solution.py:41
  365.2 4.8 %all-to-all-start.6 = ((bf16[128,1,12,128]{3,2,1,0:T(8,128)(2,1)}), bf16[128,1,12,128]{3,2,1,0:T(8,128)(2,1)S(1)}, u32[]{:S(2)}, u32[]{:S(2)}) async-start(bf16[128,1,12,128]{3,2,1,0:T(8,128)(2,1)} %copy.54), calls=%async_computation.6 | async-start | bytes 1048576 | tf_op jit(solution)/shard_map/all_to_all | solution.py:42
  370.0 1.6 fusion.8
  371.5 1.2 copy.58
  372.7 14.7 %all-to-all-done.6 = bf16[128,1,12,128]{3,2,1,0:T(8,128)(2,1)S(1)} async-done(((bf16[128,1,12,128]{3,2,1,0:T(8,128)(2,1)}), bf16[128,1,12,128]{3,2,1,0:T(8,128)(2,1)S(1)}, u32[]{:S(2)}, u32[]{:S(2)}) %all-to-all-start.6) | async-done | bytes 393248 | tf_op jit(solution)/shard_map/all_to_all | solution.py:42
  387.5 4.7 %all-to-all-start.7 = ((bf16[128,1,12,128]{3,2,1,0:T(8,128)(2,1)}), bf16[128,1,12,128]{3,2,1,0:T(8,128)(2,1)S(1)}, u32[]{:S(2)}, u32[]{:S(2)}) async-start(bf16[128,1,12,128]{3,2,1,0:T(8,128)(2,1)} %copy.58), calls=%async_computation.7 | async-start | bytes 1048576 | tf_op jit(solution)/shard_map/all_to_all | solution.py:43
  394.1 15.7 %all-to-all-done.7 = bf16[128,1,12,128]{3,2,1,0:T(8,128)(2,1)S(1)} async-done(((bf16[128,1,12,128]{3,2,1,0:T(8,128)(2,1)}), bf16[128,1,12,128]{3,2,1,0:T(8,128)(2,1)S(1)}, u32[]{:S(2)}, u32[]{:S(2)}) %all-to-all-start.7) | async-done | bytes 393248 | tf_op jit(solution)/shard_map/all_to_all | solution.py:43
  (21 shorter events, 8.8 us)
Async XLA Ops:
  0.6 300.9 %copy-start = (bf16[4,32,3072]{2,1,0:T(8,128)(2,1)S(1)}, bf16[4,32,3072]{2,1,0:T(8,128)(2,1)}, u32[]{:S(2)}) copy-start(bf16[4,32,3072]{2,1,0:T(8,128)(2,1)} %param.8) | copy-start | bytes 2359300
  2.7 30.5 %all-to-all-start.4 = ((bf16[4,32,12,128]{3,2,0,1:T(8,128)(2,1)}), bf16[4,32,12,128]{3,2,0,1:T(8,128)(2,1)S(1)}, u32[]{:S(2)}, u32[]{:S(2)}) async-start(bf16[4,32,12,128]{3,2,0,1:T(8,128)(2,1)} %copy.45), calls=%async_computation.4 | async-start | bytes 1048576 | tf_op jit(solution)/shard_map/all_to_all | solution.py:64
  61.2 7.2 %copy-start.1 = (bf16[4,32,12,128]{3,1,2,0:T(8,128)(2,1)S(1)}, bf16[4,32,12,128]{3,1,2,0:T(8,128)(2,1)}, u32[]{:S(2)}) copy-start(bf16[4,32,12,128]{3,1,2,0:T(8,128)(2,1)} %param.6) | copy-start | bytes 1179652
  61.2 218.9 %all-to-all-start.2 = ((bf16[16,96,3072]{2,1,0:T(8,128)(2,1)}), bf16[16,96,3072]{2,1,0:T(8,128)(2,1)}, u32[]{:S(2)}, u32[]{:S(2)}) async-start(bf16[16,96,3072]{2,1,0:T(8,128)(2,1)} %stack.2), calls=%async_computation.2 | async-start | bytes 18874368 | tf_op jit(solution)/shard_map/all_to_all | solution.py:54
  280.1 38.5 %all-to-all-start.1 = ((bf16[4,32,12,128]{3,2,0,1:T(8,128)(2,1)}), bf16[4,32,12,128]{3,2,0,1:T(8,128)(2,1)S(1)}, u32[]{:S(2)}, u32[]{:S(2)}) async-start(bf16[4,32,12,128]{3,2,0,1:T(8,128)(2,1)} %copy.41), calls=%async_computation.1 | async-start | bytes 1048576 | tf_op jit(solution)/shard_map/all_to_all | solution.py:63
  318.6 19.6 %all-to-all-start.3 = ((bf16[4,32,12,128]{3,0,2,1:T(4,128)(2,1)}), bf16[4,32,12,128]{3,0,2,1:T(4,128)(2,1)S(1)}, u32[]{:S(2)}, u32[]{:S(2)}) async-start(bf16[4,32,12,128]{3,0,2,1:T(4,128)(2,1)} %copy.43), calls=%async_computation.3 | async-start | bytes 786432 | tf_op jit(solution)/shard_map/all_to_all | solution.py:65
  343.0 22.2 %all-to-all-start.5 = ((bf16[128,1,12,128]{3,2,1,0:T(8,128)(2,1)}), bf16[128,1,12,128]{3,2,1,0:T(8,128)(2,1)S(1)}, u32[]{:S(2)}, u32[]{:S(2)}) async-start(bf16[128,1,12,128]{3,2,1,0:T(8,128)(2,1)} %copy.51), calls=%async_computation.5 | async-start | bytes 1048576 | tf_op jit(solution)/shard_map/all_to_all | solution.py:41
  365.2 22.3 %all-to-all-start.6 = ((bf16[128,1,12,128]{3,2,1,0:T(8,128)(2,1)}), bf16[128,1,12,128]{3,2,1,0:T(8,128)(2,1)S(1)}, u32[]{:S(2)}, u32[]{:S(2)}) async-start(bf16[128,1,12,128]{3,2,1,0:T(8,128)(2,1)} %copy.54), calls=%async_computation.6 | async-start | bytes 1048576 | tf_op jit(solution)/shard_map/all_to_all | solution.py:42
  387.5 22.3 %all-to-all-start.7 = ((bf16[128,1,12,128]{3,2,1,0:T(8,128)(2,1)}), bf16[128,1,12,128]{3,2,1,0:T(8,128)(2,1)S(1)}, u32[]{:S(2)}, u32[]{:S(2)}) async-start(bf16[128,1,12,128]{3,2,1,0:T(8,128)(2,1)} %copy.58), calls=%async_computation.7 | async-start | bytes 1048576 | tf_op jit(solution)/shard_map/all_to_all | solution.py:43
